TPU v7x, 256 devices: a whole 4x4x8 slice. The times are simulated.
256 devices in a mesh: branch: 2 (over core), gi: 16 (over y_hi, z), gj: 8 (over x, y_lo).
Axes of the slice: x: 4, y: 4 (y_hi: 2, y_lo: 2; y = y_hi * 2 + y_lo), z: 8, core: 2. Of those that a mesh axis runs over, the one named last changes fastest.
Arguments:
- homolog_embedding: float32 [128, 256, 256], P(('branch', 'gj'), 'gi'), may hold values from -6 to 6
- pair_input_tensor: float32 [256, 256, 128], P('gi', ('branch', 'gj')), may hold values from -6 to 6
- layernorm_scales: float32 [4, 256], replicated, may hold values from 0.5 to 1.5
- pair_norm_gains: float32 [3, 128], replicated, may hold values from 0.5 to 1.5
- pair_bias_matrix: float32 [128, 8], replicated
- horizontal_qkvg_kernel: float32 [256, 1024], replicated, may hold values from -0.375 to 0.375
- horizontal_final_kernel: float32 [256, 256], replicated, may hold values from -0.375 to 0.375
- vertical_qkvg_kernel: float32 [256, 1024], replicated, may hold values from -0.375 to 0.375
- vertical_final_kernel: float32 [256, 256], replicated, may hold values from -0.375 to 0.375
- feedforward_expand_kernel: float32 [256, 1024], replicated, may hold values from -0.375 to 0.375
- feedforward_shrink_kernel: float32 [1024, 256], replicated, may hold values from -0.1875 to 0.1875
- dyadic_sides_kernel: float32 [256, 64], replicated, may hold values from -0.375 to 0.375
- outer_output_matrix: float32 [1024, 128], replicated, may hold values from -1 to 1
- triangle_input_matrix: float32 [128, 640], replicated, may hold values from -0.5 to 0.5
- triangle_output_matrix: float32 [128, 128], replicated, may hold values from -0.5 to 0.5
Outputs:
- alignment_output: float32 [128, 256, 256], P(('branch', 'gj'), 'gi')
- pair_output_tensor: float32 [256, 256, 128], P('gi', ('branch', 'gj'))
All inputs are finite; a program needn't handle non-finite values.
Results may differ from a plain program's by a relative error of at most 0.0003.
Values sent between devices are 32-bit elements; how exact they have to be, the bound alone decides.
A program may use at most 64 MiB of HBM per device.

v0:
```python
import math
import jax
import jax.numpy as jnp
from jax import lax
from jax.sharding import PartitionSpec as P

epsilon = 1e-05
highest = lax.Precision.HIGHEST
lowest_start = -1e30


def from_root(shard, axis, root):
    mine = lax.axis_index(axis) == root
    return lax.psum(jnp.where(mine, shard, jnp.zeros_like(shard)), axis)


def layer_normalise(values, norm_gain):
    average = jnp.mean(values, axis=-1, keepdims=True)
    centred = values - average
    variance = jnp.mean(centred * centred, axis=-1, keepdims=True)
    return centred * lax.rsqrt(variance + epsilon) * norm_gain


def apply_projection(values, weight):
    return jnp.einsum("...c,cd->...d", values, weight, precision=highest)


def transition_update(values, norm_gain, feedforward_expand_kernel, feedforward_shrink_kernel):
    expanded = jax.nn.relu(
        apply_projection(layer_normalise(values, norm_gain), feedforward_expand_kernel)
    )
    return values + apply_projection(expanded, feedforward_shrink_kernel)


def online_update(state_carry, scores, values, einsum_form):
    running_max, sum_weights, numerator = state_carry
    new_max = jnp.maximum(running_max, jnp.max(scores, axis=-1))
    weights = jnp.exp(scores - new_max[..., None])
    sum_weights = jnp.sum(weights, axis=-1)
    numerator = jnp.einsum(einsum_form, weights, values, precision=highest)
    return (new_max, sum_weights, numerator)


def empty_state(leading, head_size):
    return (
        jnp.full(leading, lowest_start, jnp.float32),
        jnp.zeros(leading, jnp.float32),
        jnp.zeros(leading + (head_size,), jnp.float32),
    )


def panels(first_local, second_local):
    groups = lax.axis_size("gi") // lax.axis_size(("branch", "gj"))
    col_index = lax.axis_index(("branch", "gj"))
    first_panel, second_panel = (
        lax.all_gather(first_local, ("branch", "gj"), axis=1, tiled=True),
        lax.all_gather(second_local, ("branch", "gj"), axis=1, tiled=True),
    )
    pieces = from_root(second_panel, "gi", col_index * groups + 0)
    return (first_panel, pieces)


def per_device(
    homolog_embedding,
    pair_input_tensor,
    layernorm_scales,
    pair_norm_gains,
    pair_bias_matrix,
    horizontal_qkvg_kernel,
    horizontal_final_kernel,
    vertical_qkvg_kernel,
    vertical_final_kernel,
    feedforward_expand_kernel,
    feedforward_shrink_kernel,
    dyadic_sides_kernel,
    outer_output_matrix,
    triangle_input_matrix,
    triangle_output_matrix,
):
    rows_per_device, residues_per_device, alignment_width = homolog_embedding.shape
    pair_cols, pair_width = (pair_input_tensor.shape[1], pair_input_tensor.shape[2])
    head_count = pair_bias_matrix.shape[1]
    inner_feature_width = horizontal_final_kernel.shape[0]
    head_size = inner_feature_width // head_count
    outer_width = dyadic_sides_kernel.shape[1] // 2
    bias_local = apply_projection(
        layer_normalise(pair_input_tensor, pair_norm_gains[0]), pair_bias_matrix
    ).reshape(residues_per_device, pair_cols * head_count)
    bias_rows = lax.all_gather(bias_local, ("branch", "gj"), axis=1, tiled=True).reshape(
        residues_per_device, -1, head_count
    )
    bias_heads = jnp.transpose(bias_rows, (2, 0, 1))
    alignment_normalised = layer_normalise(homolog_embedding, layernorm_scales[0])
    row_query_values = apply_projection(
        alignment_normalised, horizontal_qkvg_kernel[:, :inner_feature_width]
    ).reshape(rows_per_device, residues_per_device, head_count, head_size)
    row_gate_values = apply_projection(
        alignment_normalised, horizontal_qkvg_kernel[:, 3 * inner_feature_width :]
    )
    row_start = empty_state((rows_per_device, head_count, residues_per_device), head_size)
    row_pair_slice = apply_projection(
        alignment_normalised,
        horizontal_qkvg_kernel[:, inner_feature_width : 3 * inner_feature_width],
    )
    pieces = (
        lax.all_gather(row_pair_slice[..., :inner_feature_width], "gi", axis=1, tiled=True),
        lax.all_gather(row_pair_slice[..., inner_feature_width:], "gi", axis=1, tiled=True),
    )
    key_flat = pieces[0]
    block_rows = key_flat.shape[1]
    key_block = key_flat.reshape(rows_per_device, block_rows, head_count, head_size)
    value_block = pieces[1].reshape(rows_per_device, block_rows, head_count, head_size)
    scores = (
        jnp.einsum("sihd,sjhd->shij", row_query_values, key_block, precision=highest)
        / math.sqrt(head_size)
        + bias_heads[None]
    )
    row_state = online_update(row_start, scores, value_block, "shij,sjhd->shid")
    row_heads = row_state[2] / row_state[1][..., None]
    row_attention_result = jnp.transpose(row_heads, (0, 2, 1, 3)).reshape(
        rows_per_device, residues_per_device, inner_feature_width
    )
    alignment_after_rows = homolog_embedding + apply_projection(
        jax.nn.sigmoid(row_gate_values) * row_attention_result, horizontal_final_kernel
    )
    column_normalised = layer_normalise(alignment_after_rows, layernorm_scales[1])
    column_query = apply_projection(
        column_normalised, vertical_qkvg_kernel[:, :inner_feature_width]
    ).reshape(rows_per_device, residues_per_device, head_count, head_size)
    column_pairs = apply_projection(
        column_normalised, vertical_qkvg_kernel[:, inner_feature_width : 3 * inner_feature_width]
    )
    column_gate_values = apply_projection(
        column_normalised, vertical_qkvg_kernel[:, 3 * inner_feature_width :]
    )
    column_start = empty_state((residues_per_device, head_count, rows_per_device), head_size)
    pieces = (
        lax.all_gather(
            column_pairs[..., :inner_feature_width], ("branch", "gj"), axis=0, tiled=True
        ),
        lax.all_gather(
            column_pairs[..., inner_feature_width:], ("branch", "gj"), axis=0, tiled=True
        ),
    )
    block_rows = pieces[0].shape[0]
    key_block = pieces[0].reshape(block_rows, residues_per_device, head_count, head_size)
    value_block = pieces[1].reshape(block_rows, residues_per_device, head_count, head_size)
    scores = jnp.einsum("sihd,tihd->ihst", column_query, key_block, precision=highest) / math.sqrt(
        head_size
    )
    column_state = online_update(column_start, scores, value_block, "ihst,tihd->ihsd")
    column_heads = column_state[2] / column_state[1][..., None]
    column_attention_result = jnp.transpose(column_heads, (2, 0, 1, 3)).reshape(
        rows_per_device, residues_per_device, inner_feature_width
    )
    alignment_after_columns = alignment_after_rows + apply_projection(
        jax.nn.sigmoid(column_gate_values) * column_attention_result, vertical_final_kernel
    )
    alignment_output = transition_update(
        alignment_after_columns,
        layernorm_scales[2],
        feedforward_expand_kernel,
        feedforward_shrink_kernel,
    )
    factor_pair = apply_projection(
        layer_normalise(alignment_output, layernorm_scales[3]), dyadic_sides_kernel
    )
    left_local = jnp.transpose(factor_pair[..., :outer_width], (1, 0, 2)).reshape(
        residues_per_device, rows_per_device * outer_width
    )
    right_local = jnp.transpose(factor_pair[..., outer_width:], (1, 0, 2)).reshape(
        residues_per_device, rows_per_device * outer_width
    )
    left_panel, right_panel = panels(left_local, right_local)
    all_rows = left_panel.shape[1] // outer_width
    left_three = left_panel.reshape(residues_per_device, all_rows, outer_width)
    right_three = right_panel.reshape(pair_cols, all_rows, outer_width)
    outer = jnp.einsum("isc,jsd->ijcd", left_three, right_three, precision=highest) / all_rows
    pair_first = pair_input_tensor + apply_projection(
        outer.reshape(residues_per_device, pair_cols, outer_width * outer_width),
        outer_output_matrix,
    )
    projected_values = apply_projection(
        layer_normalise(pair_first, pair_norm_gains[1]), triangle_input_matrix
    )
    left_tri = (
        jax.nn.sigmoid(projected_values[..., pair_width : 2 * pair_width])
        * projected_values[..., :pair_width]
    )
    right_tri = (
        jax.nn.sigmoid(projected_values[..., 3 * pair_width : 4 * pair_width])
        * projected_values[..., 2 * pair_width : 3 * pair_width]
    )
    out_gate = projected_values[..., 4 * pair_width :]
    left_rows, right_rows = panels(
        left_tri.reshape(residues_per_device, pair_cols * pair_width),
        right_tri.reshape(residues_per_device, pair_cols * pair_width),
    )
    left_rows = left_rows.reshape(residues_per_device, -1, pair_width)
    right_rows = right_rows.reshape(pair_cols, -1, pair_width)
    product = jnp.einsum("ikc,jkc->ijc", left_rows, right_rows, precision=highest)
    pair_output_tensor = pair_first + jax.nn.sigmoid(out_gate) * apply_projection(
        layer_normalise(product, pair_norm_gains[2]), triangle_output_matrix
    )
    return (alignment_output, pair_output_tensor)


def solution(mesh):
    return jax.shard_map(
        per_device,
        mesh=mesh,
        in_specs=(
            P(("branch", "gj"), "gi", None),
            P("gi", ("branch", "gj"), None),
            P(),
            P(),
            P(),
            P(),
            P(),
            P(),
            P(),
            P(),
            P(),
            P(),
            P(),
            P(),
            P(),
        ),
        out_specs=(P(("branch", "gj"), "gi", None), P("gi", ("branch", "gj"), None)),
        check_vma=False,
    )
```

profile of v0, /device:TPU:2, one launch (start us, length us, event | category | flops | bytes accessed | tf_op | source)
XLA Modules:
  0.0 740.1 jit_solution(3773819482061920002)
XLA Ops:
  9.5 1.4 fusion.100
  10.8 1.6 fusion.19
  17.5 40.2 %all_gather.28 = f32[16,2048]{0,1:T(8,128)S(1)} all-gather(f32[16,128]{0,1:T(8,128)S(1)} %convolution_bitcast_fusion.2), channel_id=1, replica_groups=mesh['branch'=2,'gi'=16,'gj'=8] {'branch','gj'}, dimensions={1}, use_global_device_ids=true | all-gather | bytes 139264 | tf_op jit(solution)/shard_map/all_gather | solution.py:89
  58.1 44.4 %all-gather.7.cloned.1.call-done = f32[8,256,256]{2,1,0:T(8,128)} async-done(((f32[8,16,256]{2,1,0:T(8,128)}), f32[8,256,256]{2,1,0:T(8,128)}) %all-gather.7.cloned.1.call-update) | async-done | bytes 2097168 | tf_op jit(solution)/shard_map/all_gather | solution.py:106
  102.4 2.9 copy.90
  105.4 2.9 fusion.101
  108.7 79.0 %all-gather.9.cloned.1.call-done = f32[8,256,256]{2,1,0:T(8,128)} async-done(((f32[8,16,256]{2,1,0:T(8,128)}), f32[8,256,256]{2,1,0:T(8,128)}) %all-gather.9.cloned.1.call-update) | async-done | bytes 2097168 | tf_op jit(solution)/shard_map/all_gather | solution.py:107
  187.7 2.9 copy.94
  190.6 3.5 fusion.1
  195.9 1.3 fusion.102
  200.7 30.8 %all-gather.11.cloned.1.call-done = f32[128,16,256]{2,1,0:T(8,128)} async-done(((f32[8,16,256]{2,1,0:T(8,128)}), f32[128,16,256]{2,1,0:T(8,128)}) %all-gather.11.cloned.1.call-update) | async-done | bytes 2097168 | tf_op jit(solution)/shard_map/all_gather | solution.py:138
  231.4 2.0 copy.96
  233.4 3.2 fusion.103
  237.8 32.4 %all-gather.13.cloned.1.call-done = f32[128,16,256]{2,1,0:T(8,128)} async-done(((f32[8,16,256]{2,1,0:T(8,128)}), f32[128,16,256]{2,1,0:T(8,128)}) %all-gather.13.cloned.1.call-update) | async-done | bytes 2097168 | tf_op jit(solution)/shard_map/all_gather | solution.py:141
  270.2 2.0 copy.98
  272.2 4.5 fusion.2
  277.0 1.6 fusion.6
  281.4 28.4 %all_gather.32 = f32[16,4096]{1,0:T(8,128)S(1)} all-gather(f32[16,256]{1,0:T(8,128)S(1)} %reshape.171), channel_id=1, replica_groups=mesh['branch'=2,'gi'=16,'gj'=8] {'branch','gj'}, dimensions={1}, use_global_device_ids=true | all-gather | bytes 278528 | tf_op jit(solution)/shard_map/all_gather | solution.py:57
  311.3 28.2 %all_gather.33 = f32[16,4096]{1,0:T(8,128)S(1)} all-gather(f32[16,256]{1,0:T(8,128)S(1)} %reshape.173), channel_id=1, replica_groups=mesh['branch'=2,'gi'=16,'gj'=8] {'branch','gj'}, dimensions={1}, use_global_device_ids=true | all-gather | bytes 278528 | tf_op jit(solution)/shard_map/all_gather | solution.py:56
  339.8 128.2 %all-reduce.3.cloned.1.call-done = f32[16,128,32]{1,2,0:T(8,128)} async-done(((f32[16,128,32]{1,2,0:T(8,128)}), f32[16,128,32]{1,2,0:T(8,128)}) %all-reduce.3.cloned.1.call-update) | async-done | bytes 262160 | tf_op jit(solution)/shard_map/psum | solution.py:14
  468.1 5.9 multiply_bitcast_fusion
  473.9 5.4 copy.104
  479.3 3.8 reshape.175
  487.7 32.8 %all-gather.15.cloned.1.call-done = f32[16,32768]{1,0:T(8,128)} async-done(((f32[16,2048]{1,0:T(8,128)}), f32[16,32768]{1,0:T(8,128)}) %all-gather.15.cloned.1.call-update) | async-done | bytes 2097168 | tf_op jit(solution)/shard_map/all_gather | solution.py:57
  521.0 2.1 copy.105
  523.1 35.6 %all-gather.17.cloned.1.call-done = f32[16,32768]{1,0:T(8,128)} async-done(((f32[16,2048]{1,0:T(8,128)}), f32[16,32768]{1,0:T(8,128)}) %all-gather.17.cloned.1.call-update) | async-done | bytes 2097168 | tf_op jit(solution)/shard_map/all_gather | solution.py:56
  558.7 3.3 copy.122
  562.1 2.2 copy.106
  564.4 160.5 %all-reduce.5.cloned.1.call-done = f32[16,256,128]{1,0,2:T(8,128)} async-done(((f32[16,256,128]{1,0,2:T(8,128)}), f32[16,256,128]{1,0,2:T(8,128)}) %all-reduce.5.cloned.1.call-update) | async-done | bytes 2097168 | tf_op jit(solution)/shard_map/psum | solution.py:14
  724.8 4.6 bitcast_reduce_fusion
  729.5 1.6 copy.107
  731.4 1.9 fusion.11
  (116 shorter events, 24.4 us)
Async XLA Ops:
  7.2 272.0 %copy-start = (f32[256,1024]{1,0:T(8,128)S(1)}, f32[256,1024]{1,0:T(8,128)}, u32[]{:S(2)}) copy-start(f32[256,1024]{1,0:T(8,128)} %param.24) | copy-start | bytes 3145732
  7.2 6.9 copy-start.2
  7.2 6.7 copy-start.4
  7.2 8.5 %copy-start.15 = (f32[3,128]{1,0:T(4,128)S(1)}, f32[3,128]{1,0:T(4,128)}, u32[]{:S(2)}) copy-start(f32[3,128]{1,0:T(4,128)} %param.18) | copy-start | bytes 4612
  7.2 9.3 %copy-start.13 = (f32[128,8]{0,1:T(8,128)S(1)}, f32[128,8]{0,1:T(8,128)}, u32[]{:S(2)}) copy-start(f32[128,8]{0,1:T(8,128)} %param.19) | copy-start | bytes 12292
  7.2 95.2 %all-gather.7.cloned.1.call-start = ((), (), s32[]{:S(2)}) async-start(), calls=%async_computation | async-start | bytes 2228224 | tf_op jit(solution)/shard_map/all_gather | solution.py:106
  13.1 174.6 %all-gather.9.cloned.1.call-start = ((), (), s32[]{:S(2)}) async-start(), calls=%async_computation.1 | async-start | bytes 2228224 | tf_op jit(solution)/shard_map/all_gather | solution.py:107
  13.9 217.6 %all-gather.11.cloned.1.call-start = ((), (), s32[]{:S(2)}) async-start(), calls=%async_computation.2 | async-start | bytes 2228224 | tf_op jit(solution)/shard_map/all_gather | solution.py:138
  194.2 3.2 copy-start.7
  198.6 71.6 %all-gather.13.cloned.1.call-start = ((), (), s32[]{:S(2)}) async-start(), calls=%async_computation.3 | async-start | bytes 2228224 | tf_op jit(solution)/shard_map/all_gather | solution.py:141
  199.2 268.9 %all-reduce.3.cloned.1.call-start = ((), (), s32[]{:S(2)}) async-start(), calls=%async_computation.4 | async-start | bytes 524288 | tf_op jit(solution)/shard_map/psum | solution.py:14
  236.6 0.8 copy-start.1
  276.6 1.9 copy-start.10
  276.6 2.5 copy-start.12
  276.8 3.1 copy-start.6
  278.9 1.9 copy-start.11
  280.6 30.5 %copy-start.5 = (f32[8,16,256]{2,1,0:T(8,128)}, f32[8,16,256]{2,1,0:T(8,128)S(1)}, u32[]{:S(2)}) copy-start(f32[8,16,256]{2,1,0:T(8,128)S(1)} %get-tuple-element.26) | copy-start | bytes 393220
  311.1 209.3 %all-gather.15.cloned.1.call-start = ((), (), s32[]{:S(2)}) async-start(), calls=%async_computation.5 | async-start | bytes 2228224 | tf_op jit(solution)/shard_map/all_gather | solution.py:57
  479.3 3.8 copy-start.8
  479.3 5.1 copy-start.14
  483.1 1.3 copy-start.9
  485.2 0.9 copy-start.3
  486.9 71.9 %all-gather.17.cloned.1.call-start = ((), (), s32[]{:S(2)}) async-start(), calls=%async_computation.7 | async-start | bytes 2228224 | tf_op jit(solution)/shard_map/all_gather | solution.py:56
  487.6 237.2 %all-reduce.5.cloned.1.call-start = ((), (), s32[]{:S(2)}) async-start(), calls=%async_computation.6 | async-start | bytes 4194304 | tf_op jit(solution)/shard_map/psum | solution.py:14
  564.3 167.1 %copy-start.16 = (f32[128]{0:T(128)S(1)}, f32[128]{0:T(128)}, u32[]{:S(2)}) copy-start(f32[128]{0:T(128)} %get-tuple-element.14) | copy-start | bytes 1540
  564.3 167.1 %copy-start.17 = (f32[128,128]{1,0:T(8,128)S(1)}, f32[128,128]{1,0:T(8,128)}, u32[]{:S(2)}) copy-start(f32[128,128]{1,0:T(8,128)} %param.29) | copy-start | bytes 196612
Sparse Core Ops, SparseCore 0:
  13.3 89.1 all-gather.6
  105.6 82.0 all-gather.8
  198.7 32.7 all-gather.10
  233.7 36.3 all-gather.12
  311.2 156.7 all-reduce.2
  487.0 33.4 all-gather.14
  522.3 36.3 all-gather.16
  561.4 163.4 all-reduce.4
where the time goes:
time: 741 us; the launch traced here: 740 us
  waiting for transfers between devices  545 us (74%)
  blocking collectives  96.8 us (13%)
  local copies, waits for them, and re-layouts  39.3 us (5%)
  matrix products  39.2 us (5%)
  between operations  14.8 us (2%)
    psum x2, waiting for transfers between devices, from_root(): return lax.psum(jnp.where(mine, shard, jnp.zeros_like(shard)), axis)  289 us
    all_gather x1, waiting for transfers between devices, per_device(): lax.all_gather(row_pair_slice[..., inner_feature_width:], 'gi', axis=1, t...  79 us
    all_gather x1, waiting for transfers between devices, per_device(): lax.all_gather(row_pair_slice[..., :inner_feature_width], 'gi', axis=1, t...  44.4 us
    all_gather x1, blocking collectives, per_device(): lax.all_gather(bias_local, ('branch', 'gj'), axis=1, tiled=True)  40.2 us
    all_gather x1, waiting for transfers between devices, panels(): lax.all_gather(first_local, ('branch', 'gj'), axis=1, tiled=True)  35.6 us
    all_gather x1, waiting for transfers between devices, panels(): lax.all_gather(second_local, ('branch', 'gj'), axis=1, tiled=True)  32.8 us
    all_gather x1, waiting for transfers between devices, per_device(): lax.all_gather(column_pairs[..., inner_feature_width:], ('branch', 'gj'),...  32.4 us
    all_gather x1, waiting for transfers between devices, per_device(): lax.all_gather(column_pairs[..., :inner_feature_width], ('branch', 'gj'),...  30.8 us
  transfers between devices with their start and end apart: 8, of which 8 were waited for; matrix products, arithmetic and copies ran while one was open for 4% of the time, Pallas kernels for 0%

commit v1 on v0

--- a/solution.py
+++ b/solution.py
@@ -53,7 +53,12 @@
     groups = lax.axis_size("gi") // lax.axis_size(("branch", "gj"))
     col_index = lax.axis_index(("branch", "gj"))
     first_panel, second_panel = (
-        lax.all_gather(first_local, ("branch", "gj"), axis=1, tiled=True),
+        jnp.concatenate(
+            lax.all_to_all(
+                jnp.stack([first_local] * lax.axis_size(("branch", "gj"))), ("branch", "gj"), 0, 0
+            ),
+            axis=1,
+        ),
         lax.all_gather(second_local, ("branch", "gj"), axis=1, tiled=True),
     )
     pieces = from_root(second_panel, "gi", col_index * groups + 0)

time: 741 us -> 707 us (0.954)
  waiting for transfers between devices: 545 us -> 494 us
  blocking collectives: 96.8 us -> 116 us
    all_to_all x0 -> x2, blocking collectives: none -> 47 us  [panels(): lax.all_to_all(jnp.stack([first_local] * lax.axis_size(('branch', 'gj')))...]
    all_gather x1 -> x0, waiting for transfers between devices: 35.6 us -> none  [panels(): lax.all_gather(first_local, ('branch', 'gj'), axis=1, tiled=True)]
    all_gather x1 -> x0, blocking collectives: 28.2 us -> none  [panels(): lax.all_gather(first_local, ('branch', 'gj'), axis=1, tiled=True)]
    psum x2, waiting for transfers between devices: 289 us -> 273 us  [from_root(): return lax.psum(jnp.where(mine, shard, jnp.zeros_like(shard)), axis)]
  transfers between devices with their start and end apart: 8 -> 7, of which waited for: 8 -> 7; matrix products, arithmetic and copies ran while one was open for 4% -> 3% of each run, Pallas kernels for 0% -> 0%
where the time goes in v1:
time: 707 us; the launch traced here: 706 us
  waiting for transfers between devices  494 us (70%)
  blocking collectives  116 us (16%)
  matrix products  39.3 us (6%)
  local copies, waits for them, and re-layouts  37.5 us (5%)
  between operations  14.8 us (2%)
    psum x2, waiting for transfers between devices, from_root(): return lax.psum(jnp.where(mine, shard, jnp.zeros_like(shard)), axis)  273 us
    all_gather x1, waiting for transfers between devices, per_device(): lax.all_gather(row_pair_slice[..., inner_feature_width:], 'gi', axis=1, t...  79 us
    all_to_all x2, blocking collectives, panels(): lax.all_to_all(jnp.stack([first_local] * lax.axis_size(('branch', 'gj')))...  47 us
    all_gather x1, waiting for transfers between devices, per_device(): lax.all_gather(row_pair_slice[..., :inner_feature_width], 'gi', axis=1, t...  44.2 us
    all_gather x1, blocking collectives, per_device(): lax.all_gather(bias_local, ('branch', 'gj'), axis=1, tiled=True)  40.4 us
    all_gather x1, waiting for transfers between devices, panels(): lax.all_gather(second_local, ('branch', 'gj'), axis=1, tiled=True)  33.5 us
    all_gather x1, waiting for transfers between devices, per_device(): lax.all_gather(column_pairs[..., inner_feature_width:], ('branch', 'gj'),...  32.4 us
    all_gather x1, waiting for transfers between devices, per_device(): lax.all_gather(column_pairs[..., :inner_feature_width], ('branch', 'gj'),...  30.8 us
  transfers between devices with their start and end apart: 7, of which 7 were waited for; matrix products, arithmetic and copies ran while one was open for 3% of the time, Pallas kernels for 0%

profile of v1, /device:TPU:2, one launch (start us, length us, event | category | flops | bytes accessed | tf_op | source)
XLA Modules:
  0.0 706.1 jit_solution(1328618393988036790)
XLA Ops:
  9.5 1.4 fusion.100
  10.8 1.6 fusion.19
  17.4 40.4 %all_gather.22 = f32[16,2048]{0,1:T(8,128)S(1)} all-gather(f32[16,128]{0,1:T(8,128)S(1)} %convolution_bitcast_fusion.2), channel_id=1, replica_groups=mesh['branch'=2,'gi'=16,'gj'=8] {'branch','gj'}, dimensions={1}, use_global_device_ids=true | all-gather | bytes 139264 | tf_op jit(solution)/shard_map/all_gather | solution.py:94
  58.2 44.2 %all-gather.6.cloned.1.call-done = f32[8,256,256]{2,1,0:T(8,128)} async-done(((f32[8,16,256]{2,1,0:T(8,128)}), f32[8,256,256]{2,1,0:T(8,128)}) %all-gather.6.cloned.1.call-update) | async-done | bytes 2097168 | tf_op jit(solution)/shard_map/all_gather | solution.py:111
  102.4 2.9 copy.94
  105.3 2.9 fusion.101
  108.6 79.0 %all-gather.8.cloned.1.call-done = f32[8,256,256]{2,1,0:T(8,128)} async-done(((f32[8,16,256]{2,1,0:T(8,128)}), f32[8,256,256]{2,1,0:T(8,128)}) %all-gather.8.cloned.1.call-update) | async-done | bytes 2097168 | tf_op jit(solution)/shard_map/all_gather | solution.py:112
  187.7 2.9 copy.98
  190.5 3.5 fusion.1
  195.8 1.3 fusion.102
  200.6 30.8 %all-gather.10.cloned.1.call-done = f32[128,16,256]{2,1,0:T(8,128)} async-done(((f32[8,16,256]{2,1,0:T(8,128)}), f32[128,16,256]{2,1,0:T(8,128)}) %all-gather.10.cloned.1.call-update) | async-done | bytes 2097168 | tf_op jit(solution)/shard_map/all_gather | solution.py:143
  231.4 2.0 copy.100
  233.4 3.2 fusion.103
  237.7 32.4 %all-gather.12.cloned.1.call-done = f32[128,16,256]{2,1,0:T(8,128)} async-done(((f32[8,16,256]{2,1,0:T(8,128)}), f32[128,16,256]{2,1,0:T(8,128)}) %all-gather.12.cloned.1.call-update) | async-done | bytes 2097168 | tf_op jit(solution)/shard_map/all_gather | solution.py:146
  270.1 2.0 copy.102
  272.1 4.5 fusion.2
  276.9 1.6 fusion.6
  281.3 28.3 %all_gather.26 = f32[16,4096]{1,0:T(8,128)S(1)} all-gather(f32[16,256]{1,0:T(8,128)S(1)} %reshape.169), channel_id=1, replica_groups=mesh['branch'=2,'gi'=16,'gj'=8] {'branch','gj'}, dimensions={1}, use_global_device_ids=true | all-gather | bytes 278528 | tf_op jit(solution)/shard_map/all_gather | solution.py:62
  311.2 11.1 %all_to_all.10 = f32[16,16,256]{2,1,0:T(8,128)S(1)} all-to-all(f32[16,16,256]{2,1,0:T(8,128)S(1)} %stack.6), channel_id=1, replica_groups=mesh['branch'=2,'gi'=16,'gj'=8] {'branch','gj'}, dimensions={0} | all-to-all | bytes 524288 | tf_op jit(solution)/shard_map/all_to_all | solution.py:57
  322.7 145.2 %all-reduce.3.cloned.1.call-done = f32[16,128,32]{1,2,0:T(8,128)} async-done(((f32[16,128,32]{1,2,0:T(8,128)}), f32[16,128,32]{1,2,0:T(8,128)}) %all-reduce.3.cloned.1.call-update) | async-done | bytes 262160 | tf_op jit(solution)/shard_map/psum | solution.py:14
  468.0 5.9 multiply_bitcast_fusion
  473.8 5.4 copy.109
  479.2 3.8 reshape.172
  486.0 33.5 %all-gather.14.cloned.1.call-done = f32[16,32768]{1,0:T(8,128)} async-done(((f32[16,2048]{1,0:T(8,128)}), f32[16,32768]{1,0:T(8,128)}) %all-gather.14.cloned.1.call-update) | async-done | bytes 2097168 | tf_op jit(solution)/shard_map/all_gather | solution.py:62
  520.1 2.0 copy.110
  522.4 35.9 %all_to_all.11 = f32[16,16,2048]{2,1,0:T(8,128)S(1)} all-to-all(f32[16,16,2048]{2,1,0:T(8,128)S(1)} %stack.7), channel_id=1, replica_groups=mesh['branch'=2,'gi'=16,'gj'=8] {'branch','gj'}, dimensions={0} | all-to-all | bytes 4194304 | tf_op jit(solution)/shard_map/all_to_all | solution.py:57
  559.6 1.5 reshape_reshape.7
  561.1 2.2 copy.112
  563.4 127.4 %all-reduce.5.cloned.1.call-done = f32[16,256,128]{1,0,2:T(8,128)} async-done(((f32[16,256,128]{1,0,2:T(8,128)}), f32[16,256,128]{1,0,2:T(8,128)}) %all-reduce.5.cloned.1.call-update) | async-done | bytes 2097168 | tf_op jit(solution)/shard_map/psum | solution.py:14
  690.7 4.7 bitcast_reduce_fusion
  695.5 1.6 copy.113
  697.4 1.9 fusion.11
  (120 shorter events, 24.4 us)
Async XLA Ops:
  7.2 271.9 %copy-start = (f32[256,1024]{1,0:T(8,128)S(1)}, f32[256,1024]{1,0:T(8,128)}, u32[]{:S(2)}) copy-start(f32[256,1024]{1,0:T(8,128)} %param.24) | copy-start | bytes 3145732
  7.2 6.9 copy-start.3
  7.2 6.7 copy-start.5
  7.2 8.5 %copy-start.16 = (f32[3,128]{1,0:T(4,128)S(1)}, f32[3,128]{1,0:T(4,128)}, u32[]{:S(2)}) copy-start(f32[3,128]{1,0:T(4,128)} %param.18) | copy-start | bytes 4612
  7.2 9.2 %copy-start.14 = (f32[128,8]{0,1:T(8,128)S(1)}, f32[128,8]{0,1:T(8,128)}, u32[]{:S(2)}) copy-start(f32[128,8]{0,1:T(8,128)} %param.19) | copy-start | bytes 12292
  7.2 95.1 %all-gather.6.cloned.1.call-start = ((), (), s32[]{:S(2)}) async-start(), calls=%async_computation.2 | async-start | bytes 2228224 | tf_op jit(solution)/shard_map/all_gather | solution.py:111
  13.1 174.5 %all-gather.8.cloned.1.call-start = ((), (), s32[]{:S(2)}) async-start(), calls=%async_computation.3 | async-start | bytes 2228224 | tf_op jit(solution)/shard_map/all_gather | solution.py:112
  13.9 217.5 %all-gather.10.cloned.1.call-start = ((), (), s32[]{:S(2)}) async-start(), calls=%async_computation.4 | async-start | bytes 2228224 | tf_op jit(solution)/shard_map/all_gather | solution.py:143
  194.1 3.2 copy-start.8
  198.5 71.6 %all-gather.12.cloned.1.call-start = ((), (), s32[]{:S(2)}) async-start(), calls=%async_computation.5 | async-start | bytes 2228224 | tf_op jit(solution)/shard_map/all_gather | solution.py:146
  199.1 268.9 %all-reduce.3.cloned.1.call-start = ((), (), s32[]{:S(2)}) async-start(), calls=%async_computation.6 | async-start | bytes 524288 | tf_op jit(solution)/shard_map/psum | solution.py:14
  236.5 0.8 copy-start.2
  276.5 1.9 copy-start.11
  276.6 2.5 copy-start.13
  276.7 3.2 copy-start.7
  278.9 1.9 copy-start.12
  280.5 30.5 %copy-start.6 = (f32[8,16,256]{2,1,0:T(8,128)}, f32[8,16,256]{2,1,0:T(8,128)S(1)}, u32[]{:S(2)}) copy-start(f32[8,16,256]{2,1,0:T(8,128)S(1)} %get-tuple-element.26) | copy-start | bytes 393220
  311.0 208.5 %all-gather.14.cloned.1.call-start = ((), (), s32[]{:S(2)}) async-start(), calls=%async_computation.7 | async-start | bytes 2228224 | tf_op jit(solution)/shard_map/all_gather | solution.py:62
  479.2 3.8 copy-start.9
  479.2 5.1 copy-start.15
  483.0 1.3 copy-start.10
  485.1 34.6 %copy-start.4 = (f32[16,16,640]{2,1,0:T(8,128)}, f32[16,16,640]{2,1,0:T(8,128)S(1)}, u32[]{:S(2)}) copy-start(f32[16,16,640]{2,1,0:T(8,128)S(1)} %fusion.27) | copy-start | bytes 1966084
  486.0 204.7 %all-reduce.5.cloned.1.call-start = ((), (), s32[]{:S(2)}) async-start(), calls=%async_computation.8 | async-start | bytes 4194304 | tf_op jit(solution)/shard_map/psum | solution.py:14
  563.3 134.0 %copy-start.17 = (f32[128]{0:T(128)S(1)}, f32[128]{0:T(128)}, u32[]{:S(2)}) copy-start(f32[128]{0:T(128)} %get-tuple-element.14) | copy-start | bytes 1540
  563.4 134.0 %copy-start.18 = (f32[128,128]{1,0:T(8,128)S(1)}, f32[128,128]{1,0:T(8,128)}, u32[]{:S(2)}) copy-start(f32[128,128]{1,0:T(8,128)} %param.29) | copy-start | bytes 196612
  690.7 8.6 %copy-start.1 = (f32[256,1024]{1,0:T(8,128)S(1)}, f32[256,1024]{1,0:T(8,128)}, u32[]{:S(2)}) copy-start(f32[256,1024]{1,0:T(8,128)} %param.24) | copy-start | bytes 3145732
Sparse Core Ops, SparseCore 0:
  13.3 89.0 all-gather.5
  105.5 82.0 all-gather.7
  198.6 32.7 all-gather.9
  233.6 36.3 all-gather.11
  311.2 156.7 all-reduce.2
  486.1 33.3 all-gather.13
  522.3 168.3 all-reduce.4
